TPU v7x, 128 devices: a whole 4x4x4 slice. The times are simulated.
128 devices in a mesh: member: 8 (over y, core), tile: 16 (over z, x).
Axes of the slice: x: 4, y: 4, z: 4, core: 2. Of those that a mesh axis runs over, the one named last changes fastest.
Arguments:
- perturb: bfloat16 [128, 256, 2560], P('member', 'tile'), may hold values from -0.5 to 0.5
- weights: float32 [128, 64, 1280], P('member', 'tile'), may hold values from -1.2 to 1.2
- column_map: bfloat16 [1280, 2560], replicated, may hold values from -0.15625 to 0.15625
- background: float32 [256, 2560], P('tile', 'member'), may hold values from -6 to 6
- stencil_index: int32 [16, 128, 8, 8], P('tile'), may hold values from 0 to 4798, as said below
- row_fraction: float32 [16, 128, 8, 8], P('tile'), may hold values from 0 to 1
- column_fraction: float32 [16, 128, 8, 8], P('tile'), may hold values from 0 to 1
- block_lengths: int32 [16, 128, 8], P('tile'), may hold values from 0 to 8, as said below
- obs_value: float32 [128, 128, 8], P(('member', 'tile')), may hold values from -6 to 6
- obs_error: float32 [128, 128, 8], P(('member', 'tile')), may hold values from 0.3 to 1
- instrument_gain: float32 [128], P(('member', 'tile')), may hold values from 0.2 to 0.8
Outputs:
- analysis_weights: float32 [128, 64, 1280], P('member', 'tile')
- analysis_increment: float32 [256, 2560], P('tile', 'member')
Inputs may be any that keep to these rules, and one draw needn't show every extreme that they name: stencil_index = r * 320 + c with 0 <= r < 15 and 0 <= c < 319. `block_lengths`: in every draw some owner (one tile and one member index) has all its blocks full.
All inputs are finite; a program needn't handle non-finite values.
Results may differ from a plain program's by a relative error of at most 0.0022.
Values may be sent and summed in bfloat16 or wider, within the bound.
No kernel may reach another device: no remote copies, remote signals or barrier semaphores. Data moves between devices by JAX's collectives and lax.ppermute only.
A program may use at most 64 MiB of HBM per device.

v0:
```python
import jax
import jax.numpy as jnp
from jax import lax
from jax.sharding import PartitionSpec as P

RATIO = 4
KSM = 3
DIFFUSION = 0.45


def padded_2(block, sides, width):
    for axis, dim in sides:
        count = lax.axis_size(axis)
        forward = [(i, i + 1) for i in range(count - 1)]
        backward = [(target, source) for source, target in forward]
        low = lax.ppermute(
            lax.slice_in_dim(block, block.shape[dim] - width, None, axis=dim), axis, forward
        )
        high = lax.ppermute(lax.slice_in_dim(block, 0, width, axis=dim), axis, backward)
        block = jnp.concatenate([low, block, high], axis=dim)
    return block


def rows_halo(grid_values, width_rows):
    return padded_2(grid_values, (("tile", 1),), width_rows)


def smoothed(grid_values, extra_rows):
    for pass_index in range(KSM):
        padded = rows_halo(grid_values, 1)
        grid_values = grid_values + DIFFUSION * (padded[:, :-2] + padded[:, 2:] - 2.0 * grid_values)
    if extra_rows > 0:
        rounded_rows = grid_values.astype(jnp.bfloat16)
        grid_values = padded_2(rounded_rows, (("tile", 1),), extra_rows)
    return grid_values


def refine(extended):
    members_here, row_count, col_count = extended.shape
    lower_rows = extended[:, :-2]
    middle = extended[:, 1:-1]
    upper_rows = extended[:, 2:]
    pieces = []
    for offset in range(RATIO):
        shift_value = (offset + 0.5) / RATIO - 0.5
        if shift_value < 0:
            pieces.append((1.0 + shift_value) * middle - shift_value * lower_rows)
        else:
            pieces.append((1.0 - shift_value) * middle + shift_value * upper_rows)
    return jnp.stack(pieces, axis=2).reshape(members_here, (row_count - 2) * RATIO, col_count)


def refine_adjoint(fine_field):
    members_here, fine_count, col_count = fine_field.shape
    row_count = fine_count // RATIO
    blocks = fine_field.reshape(members_here, row_count, RATIO, col_count)
    middle = jnp.zeros_like(blocks[:, :, 0])
    lower_rows = jnp.zeros_like(middle)
    upper_rows = jnp.zeros_like(middle)
    for offset in range(RATIO):
        shift_value = (offset + 0.5) / RATIO - 0.5
        fine_layer = blocks[:, :, offset]
        if shift_value < 0:
            middle = middle + (1.0 + shift_value) * fine_layer
            lower_rows = lower_rows - shift_value * fine_layer
        else:
            middle = middle + (1.0 - shift_value) * fine_layer
            upper_rows = upper_rows + shift_value * fine_layer
    return (
        jnp.pad(middle, ((0, 0), (1, 1), (0, 0)))
        + jnp.pad(lower_rows, ((0, 0), (0, 2), (0, 0)))
        + jnp.pad(upper_rows, ((0, 0), (2, 0), (0, 0)))
    )


def forward(coarse, perturb, column_map):
    extended = smoothed(coarse, 1)
    members_here, row_count, coarse_cols = extended.shape
    mapped = jnp.dot(
        extended.reshape(-1, coarse_cols), column_map, preferred_element_type=jnp.float32
    )
    fine_field = refine(mapped.reshape(members_here, row_count, -1))
    member_term = jnp.sum(fine_field * perturb, axis=0)
    return lax.psum_scatter(member_term, "member", scatter_dimension=1, tiled=True)


def adjoint_map(spread_field, perturb, column_map):
    edge_terms = refine_adjoint(perturb * spread_field)
    rim_rows = jnp.stack([edge_terms[:, 0], edge_terms[:, -1]], axis=1)
    beside_all = rows_halo(rim_rows, 1)
    inner_rows = edge_terms[:, 1:-1]
    inner_rows = inner_rows.at[:, 0].add(beside_all[:, 0]).at[:, -1].add(beside_all[:, 3])
    members_here, row_count, fine_cols = inner_rows.shape
    pulled = lax.dot_general(
        inner_rows.astype(jnp.bfloat16).reshape(-1, fine_cols),
        column_map,
        (((1,), (1,)), ((), ())),
        preferred_element_type=jnp.float32,
    )
    return smoothed(pulled.reshape(members_here, row_count, -1), 0)


def bilinear_factors(index, row_frac, column_frac, region_width, row_count):
    row_pos = (index // region_width)[..., None]
    column_pos = (index % region_width)[..., None]
    row_ids = lax.broadcasted_iota(jnp.int32, index.shape + (row_count,), index.ndim)
    column_ids = lax.broadcasted_iota(jnp.int32, index.shape + (region_width,), index.ndim)
    row_factor = jnp.where(row_ids == row_pos, 1.0 - row_frac[..., None], 0.0) + jnp.where(
        row_ids == row_pos + 1, row_frac[..., None], 0.0
    )
    column_factor = jnp.where(
        column_ids == column_pos, 1.0 - column_frac[..., None], 0.0
    ) + jnp.where(column_ids == column_pos + 1, column_frac[..., None], 0.0)
    return (row_factor, column_factor)


def interpolate_region(field_region, index, row_frac, column_frac):
    row_count, region_width = field_region.shape
    row_factor, column_factor = bilinear_factors(
        index, row_frac, column_frac, region_width, row_count
    )
    along = jnp.einsum("bsr,rc->bsc", row_factor, field_region, precision=lax.Precision.HIGHEST)
    return jnp.sum(along * column_factor, axis=-1)


def spread_tile(residual, index, row_frac, column_frac, region_width, row_count):
    row_factor, column_factor = bilinear_factors(
        index, row_frac, column_frac, region_width, row_count
    )
    weighted = row_factor * residual[..., None]
    regions = jnp.einsum("bmsr,bmsc->rmc", weighted, column_factor, precision=lax.Precision.HIGHEST)
    return regions.reshape(row_count, -1)


def innovation(obs_state, obs_value, obs_error, instrument):
    bounded = jnp.tanh(obs_state)
    derivative = 1.0 + instrument * (1.0 - bounded * bounded)
    misfit = obs_state + instrument * bounded - obs_value
    precision_obs = 1.0 / (obs_error * obs_error)
    return (derivative * misfit * precision_obs, derivative * derivative * precision_obs)


def global_sum(values):
    return lax.psum(values, ("member", "tile"))


def shards(
    perturb,
    weights,
    column_map,
    background,
    stencil_index,
    row_fraction,
    column_fraction,
    block_lengths,
    obs_value,
    obs_error,
    instrument_gain,
):
    member_pos = lax.axis_index("member")
    member_count = lax.axis_size("member")
    tile_count = lax.axis_size("tile")
    fine_rows, region_width = background.shape
    local_index = stencil_index[0]
    local_row = row_fraction[0]
    local_col = column_fraction[0]
    slot_ids = lax.broadcasted_iota(jnp.int32, local_index.shape, 2)
    valid_slots = (slot_ids < block_lengths[0][:, :, None]).astype(jnp.float32)
    own_index = lax.dynamic_index_in_dim(local_index, member_pos, 1, False)
    own_row = lax.dynamic_index_in_dim(local_row, member_pos, 1, False)
    own_col = lax.dynamic_index_in_dim(local_col, member_pos, 1, False)
    own_valid = lax.dynamic_index_in_dim(valid_slots, member_pos, 1, False)

    def fan_out(values):
        arranged = jnp.transpose(values.reshape(member_count, tile_count, -1), (1, 0, 2))
        widened = jnp.broadcast_to(arranged[None], (member_count,) + arranged.shape)
        return widened.reshape(member_count * tile_count, member_count, -1)

    coarse = weights
    increment = forward(coarse, perturb, column_map)
    obs_state = interpolate_region(background + increment, own_index, own_row, own_col)
    received = lax.all_to_all(
        obs_state, ("member", "tile"), split_axis=0, concat_axis=0, tiled=True
    )
    residual, obs_weight = innovation(received, obs_value[0], obs_error[0], instrument_gain[0])
    residual, obs_weight = (
        lax.all_to_all(
            fan_out(residual), ("member", "tile"), split_axis=0, concat_axis=0, tiled=True
        ),
        lax.all_to_all(
            fan_out(obs_weight), ("member", "tile"), split_axis=0, concat_axis=0, tiled=True
        ),
    )
    spread_field = spread_tile(
        residual * valid_slots, local_index, local_row, local_col, region_width, fine_rows
    )
    gradient = coarse + adjoint_map(spread_field, perturb, column_map)
    grad_square = jnp.sum(gradient * gradient)
    grad_total = global_sum(grad_square)
    grad_image = forward(gradient, perturb, column_map)
    grad_obs = interpolate_region(grad_image, own_index, own_row, own_col)
    own_weight = lax.dynamic_index_in_dim(obs_weight, member_pos, 1, False)
    curvature = jnp.sum(own_valid * own_weight * grad_obs * grad_obs)
    curve_total = global_sum(curvature)
    step_size = grad_total / (grad_total + curve_total)
    coarse = coarse - step_size * gradient
    increment = increment - step_size * grad_image
    return (coarse, increment)


def solution(mesh):
    placed = (
        P("member", "tile", None),
        P("member", "tile", None),
        P(),
        P("tile", "member"),
        P("tile", None, None, None),
        P("tile", None, None, None),
        P("tile", None, None, None),
        P("tile", None, None),
        P(("member", "tile"), None, None),
        P(("member", "tile"), None, None),
        P(("member", "tile")),
    )
    return jax.shard_map(
        shards,
        mesh=mesh,
        in_specs=placed,
        out_specs=(P("member", "tile", None), P("tile", "member")),
        check_vma=False,
    )
```

profile of v0, /device:TPU:1, one launch (start us, length us, event | category | flops | bytes accessed | tf_op | source)
XLA Modules:
  0.0 360.1 jit_solution(11399913175671601973)
XLA Ops:
  7.2 1.0 copy.144
  8.3 3.9 %collective-permute-start = (f32[16,1,1280]{2,0,1:T(8,128)S(1)}, f32[16,1,1280]{2,0,1:T(8,128)S(1)}, u32[]{:S(2)}, u32[]{:S(2)}) collective-permute-start(f32[16,1,1280]{2,0,1:T(8,128)S(1)} %get-tuple-element.79), channel_id=1, source_target_pairs={{0,1},{1,2},{2,3},{3,4},{4,5},{5,6},{6,7},{7,8},{8,9},{9,10},{10,1... | collective-permute-start | bytes 245768 | tf_op jit(solution)/shard_map/ppermute | solution.py:16
  12.2 1.3 collective-permute-start.1
  13.7 3.7 %collective-permute-done.1 = f32[16,1,1280]{2,0,1:T(8,128)S(1)} collective-permute-done((f32[16,1,1280]{2,0,1:T(8,128)S(1)}, f32[16,1,1280]{2,0,1:T(8,128)S(1)}, u32[]{:S(2)}, u32[]{:S(2)}) %collective-permute-start.1) | collective-permute-done | bytes 81952 | tf_op jit(solution)/shard_map/ppermute | solution.py:19
  17.5 3.1 collective-permute-start.2
  20.6 1.3 collective-permute-start.3
  22.1 3.7 %collective-permute-done.3 = f32[16,1,1280]{2,0,1:T(8,128)S(1)} collective-permute-done((f32[16,1,1280]{2,0,1:T(8,128)S(1)}, f32[16,1,1280]{2,0,1:T(8,128)S(1)}, u32[]{:S(2)}, u32[]{:S(2)}) %collective-permute-start.3) | collective-permute-done | bytes 81952 | tf_op jit(solution)/shard_map/ppermute | solution.py:19
  25.9 5.0 %collective-permute-start.4 = (f32[16,1,1280]{2,0,1:T(8,128)S(1)}, f32[16,1,1280]{2,0,1:T(8,128)S(1)}, u32[]{:S(2)}, u32[]{:S(2)}) collective-permute-start(f32[16,1,1280]{2,0,1:T(8,128)S(1)} %get-tuple-element.75), channel_id=1, source_target_pairs={{0,1},{1,2},{2,3},{3,4},{4,5},{5,6},{6,7},{7,8},{8,9},{9,10},{10,1... | collective-permute-start | bytes 245768 | tf_op jit(solution)/shard_map/ppermute | solution.py:16
  30.9 1.3 collective-permute-start.5
  32.4 3.7 %collective-permute-done.5 = f32[16,1,1280]{2,0,1:T(8,128)S(1)} collective-permute-done((f32[16,1,1280]{2,0,1:T(8,128)S(1)}, f32[16,1,1280]{2,0,1:T(8,128)S(1)}, u32[]{:S(2)}, u32[]{:S(2)}) %collective-permute-start.5) | collective-permute-done | bytes 81952 | tf_op jit(solution)/shard_map/ppermute | solution.py:19
  36.2 4.0 %collective-permute-start.6 = (bf16[16,1,1280]{2,0,1:T(8,128)(2,1)S(1)}, bf16[16,1,1280]{2,0,1:T(8,128)(2,1)S(1)}, u32[]{:S(2)}, u32[]{:S(2)}) collective-permute-start(bf16[16,1,1280]{2,0,1:T(8,128)(2,1)S(1)} %get-tuple-element.83), channel_id=1, source_target_pairs={{0,1},{1,2},{2,3},{3,4},{4,5},{5,6},{6,7},{7,8},{8,9},{9,10},{10,1... | collective-permute-start | bytes 122888 | tf_op jit(solution)/shard_map/ppermute | solution.py:16
  40.2 1.3 collective-permute-start.7
  41.6 3.7 %collective-permute-done.7 = bf16[16,1,1280]{2,0,1:T(8,128)(2,1)S(1)} collective-permute-done((bf16[16,1,1280]{2,0,1:T(8,128)(2,1)S(1)}, bf16[16,1,1280]{2,0,1:T(8,128)(2,1)S(1)}, u32[]{:S(2)}, u32[]{:S(2)}) %collective-permute-start.7) | collective-permute-done | bytes 40992 | tf_op jit(solution)/shard_map/ppermute | solution.py:19
  45.2 4.0 %fusion.8 = f32[16,6,2560]{2,0,1:T(8,128)S(1)} fusion(bf16[1280,2560]{1,0:T(8,128)(2,1)} %param.17, bf16[16,1,1280]{2,0,1:T(8,128)(2,1)S(1)} %collective-permute-done.7, bf16[16,4,1280]{2,0,1:T(8,128)(2,1)S(1)} %fusion.56, bf16[16,1,1280]{2,0,1:T(8,128)(2,1)S(1)} %collective-permute-done.6), kind=kOutput, calls=%fused_computation.10 | convolution fusion | flops 629391360 | bytes 7782400 | tf_op jit(solution)/shard_map/dot_general | solution.py:79
  50.1 1.1 copy-done
  51.2 1.3 fusion.15
  52.5 1.5 copy.150
  54.1 38.6 %reduce-scatter.7.cloned.1.call-done = f32[320,16]{1,0:T(8,128)} async-done(((f32[2560,16]{1,0:T(8,128)}), f32[320,16]{1,0:T(8,128)}) %reduce-scatter.7.cloned.1.call-update) | async-done | bytes 20496
  92.6 1.0 copy.151
  93.6 1.5 fusion.17
  95.2 0.7 copy.126
  95.9 9.8 %all-to-all-start = ((f32[128,1,8]{2,1,0:T(1,128)}), f32[128,1,8]{2,1,0:T(1,128)S(1)}, u32[]{:S(2)}, u32[]{:S(2)}) async-start(f32[128,1,8]{2,1,0:T(1,128)} %copy.126), calls=%async_computation | async-start | bytes 131072 | tf_op jit(solution)/shard_map/all_to_all | solution.py:182
  106.5 8.9 %all-to-all-done = f32[128,1,8]{2,1,0:T(1,128)S(1)} async-done(((f32[128,1,8]{2,1,0:T(1,128)}), f32[128,1,8]{2,1,0:T(1,128)S(1)}, u32[]{:S(2)}, u32[]{:S(2)}) %all-to-all-start) | async-done | bytes 4128 | tf_op jit(solution)/shard_map/all_to_all | solution.py:182
  115.7 0.8 broadcast_in_dim.136
  116.5 4.3 %all-to-all-start.1 = ((f32[128,8,8]{2,1,0:T(8,128)}), f32[128,8,8]{2,1,0:T(8,128)S(1)}, u32[]{:S(2)}, u32[]{:S(2)}) async-start(f32[128,8,8]{2,1,0:T(8,128)} %bitcast.22), calls=%async_computation.1 | async-start | bytes 1048576 | tf_op jit(solution)/shard_map/all_to_all | solution.py:187
  120.8 14.1 %all-to-all-done.1 = f32[128,8,8]{2,1,0:T(8,128)S(1)} async-done(((f32[128,8,8]{2,1,0:T(8,128)}), f32[128,8,8]{2,1,0:T(8,128)S(1)}, u32[]{:S(2)}, u32[]{:S(2)}) %all-to-all-start.1) | async-done | bytes 32800 | tf_op jit(solution)/shard_map/all_to_all | solution.py:187
  135.1 11.3 %fusion.19 = f32[16,8,320]{2,0,1:T(8,128)S(1)} fusion(f32[128,8,8]{0,2,1:T(8,128)S(1)} %bitcast.162, s32[128,8,8]{0,2,1:T(8,128)S(1)} %get-tuple-element.89, f32[128,8,8]{0,2,1:T(8,128)S(1)} %get-tuple-element.96, s32[128,8,8]{0,2,1:T(8,128)S(1)} %get-tuple-element.90, f32[128,8,8]{0,2,1:T(8,128)S(1)} %broadcast_select_fusion, ...), kind=kOutput, calls=%fused_computation.31 | convolution fusion | flops 517210112 | bytes 458752 | tf_op jit(solution)/shard_map/bmsr,bmsc->rmc/dot_general | solution.py:131
  146.7 0.8 convert_multiply_fusion.1
  147.9 2.4 collective-permute-start.8
  150.4 1.5 collective-permute-start.9
  152.0 1.3 collective-permute-done.8
  153.3 3.9 %collective-permute-done.9 = f32[16,1,2560]{2,0,1:T(8,128)S(1)} collective-permute-done((f32[16,1,2560]{2,0,1:T(8,128)S(1)}, f32[16,1,2560]{2,0,1:T(8,128)S(1)}, u32[]{:S(2)}, u32[]{:S(2)}) %collective-permute-start.9) | collective-permute-done | bytes 163872 | tf_op jit(solution)/shard_map/ppermute | solution.py:19
  157.3 2.1 fusion.6
  159.4 2.6 collective-permute-start.10
  162.0 1.3 collective-permute-start.11
  163.5 3.7 %collective-permute-done.11 = f32[16,1,1280]{2,0,1:T(8,128)S(1)} collective-permute-done((f32[16,1,1280]{2,0,1:T(8,128)S(1)}, f32[16,1,1280]{2,0,1:T(8,128)S(1)}, u32[]{:S(2)}, u32[]{:S(2)}) %collective-permute-start.11) | collective-permute-done | bytes 81952 | tf_op jit(solution)/shard_map/ppermute | solution.py:19
  167.3 3.9 %collective-permute-start.12 = (f32[16,1,1280]{2,0,1:T(8,128)S(1)}, f32[16,1,1280]{2,0,1:T(8,128)S(1)}, u32[]{:S(2)}, u32[]{:S(2)}) collective-permute-start(f32[16,1,1280]{2,0,1:T(8,128)S(1)} %get-tuple-element.71), channel_id=1, source_target_pairs={{0,1},{1,2},{2,3},{3,4},{4,5},{5,6},{6,7},{7,8},{8,9},{9,10},{10,1... | collective-permute-start | bytes 245768 | tf_op jit(solution)/shard_map/ppermute | solution.py:16
  171.2 1.3 collective-permute-start.13
  172.7 3.7 %collective-permute-done.13 = f32[16,1,1280]{2,0,1:T(8,128)S(1)} collective-permute-done((f32[16,1,1280]{2,0,1:T(8,128)S(1)}, f32[16,1,1280]{2,0,1:T(8,128)S(1)}, u32[]{:S(2)}, u32[]{:S(2)}) %collective-permute-start.13) | collective-permute-done | bytes 81952 | tf_op jit(solution)/shard_map/ppermute | solution.py:19
  176.5 4.3 %collective-permute-start.14 = (f32[16,1,1280]{2,0,1:T(8,128)S(1)}, f32[16,1,1280]{2,0,1:T(8,128)S(1)}, u32[]{:S(2)}, u32[]{:S(2)}) collective-permute-start(f32[16,1,1280]{2,0,1:T(8,128)S(1)} %get-tuple-element.69), channel_id=1, source_target_pairs={{0,1},{1,2},{2,3},{3,4},{4,5},{5,6},{6,7},{7,8},{8,9},{9,10},{10,1... | collective-permute-start | bytes 245768 | tf_op jit(solution)/shard_map/ppermute | solution.py:16
  180.8 1.3 collective-permute-start.15
  182.3 3.7 %collective-permute-done.15 = f32[16,1,1280]{2,0,1:T(8,128)S(1)} collective-permute-done((f32[16,1,1280]{2,0,1:T(8,128)S(1)}, f32[16,1,1280]{2,0,1:T(8,128)S(1)}, u32[]{:S(2)}, u32[]{:S(2)}) %collective-permute-start.15) | collective-permute-done | bytes 81952 | tf_op jit(solution)/shard_map/ppermute | solution.py:19
  186.7 3.7 %collective-permute-start.16 = (f32[16,1,1280]{2,0,1:T(8,128)S(1)}, f32[16,1,1280]{2,0,1:T(8,128)S(1)}, u32[]{:S(2)}, u32[]{:S(2)}) collective-permute-start(f32[16,1,1280]{2,0,1:T(8,128)S(1)} %get-tuple-element.67), channel_id=1, source_target_pairs={{0,1},{1,2},{2,3},{3,4},{4,5},{5,6},{6,7},{7,8},{8,9},{9,10},{10,1... | collective-permute-start | bytes 245768 | tf_op jit(solution)/shard_map/ppermute | solution.py:16
  190.5 1.3 collective-permute-start.17
  191.9 3.7 %collective-permute-done.17 = f32[16,1,1280]{2,0,1:T(8,128)S(1)} collective-permute-done((f32[16,1,1280]{2,0,1:T(8,128)S(1)}, f32[16,1,1280]{2,0,1:T(8,128)S(1)}, u32[]{:S(2)}, u32[]{:S(2)}) %collective-permute-start.17) | collective-permute-done | bytes 81952 | tf_op jit(solution)/shard_map/ppermute | solution.py:19
  195.7 4.0 %collective-permute-start.18 = (f32[16,1,1280]{2,0,1:T(8,128)S(1)}, f32[16,1,1280]{2,0,1:T(8,128)S(1)}, u32[]{:S(2)}, u32[]{:S(2)}) collective-permute-start(f32[16,1,1280]{2,0,1:T(8,128)S(1)} %get-tuple-element.65), channel_id=1, source_target_pairs={{0,1},{1,2},{2,3},{3,4},{4,5},{5,6},{6,7},{7,8},{8,9},{9,10},{10,1... | collective-permute-start | bytes 245768 | tf_op jit(solution)/shard_map/ppermute | solution.py:16
  199.8 1.3 collective-permute-start.19
  201.2 3.7 %collective-permute-done.19 = f32[16,1,1280]{2,0,1:T(8,128)S(1)} collective-permute-done((f32[16,1,1280]{2,0,1:T(8,128)S(1)}, f32[16,1,1280]{2,0,1:T(8,128)S(1)}, u32[]{:S(2)}, u32[]{:S(2)}) %collective-permute-start.19) | collective-permute-done | bytes 81952 | tf_op jit(solution)/shard_map/ppermute | solution.py:19
  205.0 4.0 %collective-permute-start.20 = (f32[16,1,1280]{2,0,1:T(8,128)S(1)}, f32[16,1,1280]{2,0,1:T(8,128)S(1)}, u32[]{:S(2)}, u32[]{:S(2)}) collective-permute-start(f32[16,1,1280]{2,0,1:T(8,128)S(1)} %get-tuple-element.63), channel_id=1, source_target_pairs={{0,1},{1,2},{2,3},{3,4},{4,5},{5,6},{6,7},{7,8},{8,9},{9,10},{10,1... | collective-permute-start | bytes 245768 | tf_op jit(solution)/shard_map/ppermute | solution.py:16
  209.1 1.3 collective-permute-start.21
  210.5 3.7 %collective-permute-done.21 = f32[16,1,1280]{2,0,1:T(8,128)S(1)} collective-permute-done((f32[16,1,1280]{2,0,1:T(8,128)S(1)}, f32[16,1,1280]{2,0,1:T(8,128)S(1)}, u32[]{:S(2)}, u32[]{:S(2)}) %collective-permute-start.21) | collective-permute-done | bytes 81952 | tf_op jit(solution)/shard_map/ppermute | solution.py:19
  214.3 4.0 %collective-permute-start.22 = (bf16[16,1,1280]{2,0,1:T(8,128)(2,1)S(1)}, bf16[16,1,1280]{2,0,1:T(8,128)(2,1)S(1)}, u32[]{:S(2)}, u32[]{:S(2)}) collective-permute-start(bf16[16,1,1280]{2,0,1:T(8,128)(2,1)S(1)} %get-tuple-element.81), channel_id=1, source_target_pairs={{0,1},{1,2},{2,3},{3,4},{4,5},{5,6},{6,7},{7,8},{8,9},{9,10},{10,1... | collective-permute-start | bytes 122888 | tf_op jit(solution)/shard_map/ppermute | solution.py:16
  218.4 1.3 collective-permute-start.23
  219.8 0.8 broadcast_in_dim.138
  220.6 18.2 %all-to-all-start.2 = ((f32[128,8,8]{2,1,0:T(8,128)}), f32[128,8,8]{2,1,0:T(8,128)S(1)}, u32[]{:S(2)}, u32[]{:S(2)}) async-start(f32[128,8,8]{2,1,0:T(8,128)} %bitcast.31), calls=%async_computation.2 | async-start | bytes 1048576 | tf_op jit(solution)/shard_map/all_to_all | solution.py:190
  238.9 4.0 %fusion.4 = f32[16,6,2560]{2,0,1:T(8,128)S(1)} fusion(bf16[1280,2560]{1,0:T(8,128)(2,1)} %param.17, bf16[16,1,1280]{2,0,1:T(8,128)(2,1)S(1)} %collective-permute-done.23, bf16[16,4,1280]{2,0,1:T(8,128)(2,1)S(1)} %fusion.30, bf16[16,1,1280]{2,0,1:T(8,128)(2,1)S(1)} %collective-permute-done.22), kind=kOutput, calls=%fused_computation.6 | convolution fusion | flops 629391360 | bytes 7782400 | tf_op jit(solution)/shard_map/dot_general | solution.py:79
  243.8 1.3 fusion.16
  245.1 1.5 copy.152
  246.6 6.3 %all-to-all-done.2 = f32[128,8,8]{2,1,0:T(8,128)S(1)} async-done(((f32[128,8,8]{2,1,0:T(8,128)}), f32[128,8,8]{2,1,0:T(8,128)S(1)}, u32[]{:S(2)}, u32[]{:S(2)}) %all-to-all-start.2) | async-done | bytes 32800 | tf_op jit(solution)/shard_map/all_to_all | solution.py:190
  253.0 25.0 %reduce-scatter.9.cloned.1.call-done = f32[320,16]{1,0:T(8,128)} async-done(((f32[2560,16]{1,0:T(8,128)}), f32[320,16]{1,0:T(8,128)}) %reduce-scatter.9.cloned.1.call-update) | async-done | bytes 20496
  278.1 1.0 copy.153
  279.1 2.4 fusion.18
  282.0 67.6 %all-reduce.3 = (f32[]{:T(128)}, f32[]{:T(128)}) all-reduce(f32[]{:T(128)} %get-tuple-element.40, f32[]{:T(128)} %fusion.103), channel_id=1, replica_groups=mesh['member'=8,'tile'=16] {'member','tile'}, use_global_device_ids=true, to_apply=%region_4.5 | all-reduce | flops 2 | bytes 16 | tf_op jit(solution)/shard_map/psum | solution.py:144
  352.3 0.9 copy.145
  (91 shorter events, 7.4 us)
Async XLA Ops:
  7.2 34.4 %copy-start.2 = (s32[1,128,8,8]{1,3,2,0:T(8,128)S(1)}, s32[1,128,8,8]{1,3,2,0:T(8,128)}, u32[]{:S(2)}) copy-start(s32[1,128,8,8]{1,3,2,0:T(8,128)} %param.19) | copy-start | bytes 98308
  7.2 85.5 %reduce-scatter.7.cloned.1.call-start = ((), (), s32[]{:S(2)}) async-start(), calls=%async_computation.5 | async-start | bytes 1474560
  8.3 5.4 %collective-permute-start = (f32[16,1,1280]{2,0,1:T(8,128)S(1)}, f32[16,1,1280]{2,0,1:T(8,128)S(1)}, u32[]{:S(2)}, u32[]{:S(2)}) collective-permute-start(f32[16,1,1280]{2,0,1:T(8,128)S(1)} %get-tuple-element.79), channel_id=1, source_target_pairs={{0,1},{1,2},{2,3},{3,4},{4,5},{5,6},{6,7},{7,8},{8,9},{9,10},{10,1... | collective-permute-start | bytes 245768 | tf_op jit(solution)/shard_map/ppermute | solution.py:16
  12.2 5.2 %collective-permute-start.1 = (f32[16,1,1280]{2,0,1:T(8,128)S(1)}, f32[16,1,1280]{2,0,1:T(8,128)S(1)}, u32[]{:S(2)}, u32[]{:S(2)}) collective-permute-start(f32[16,1,1280]{2,0,1:T(8,128)S(1)} %get-tuple-element.80), channel_id=1, source_target_pairs={{1,0},{2,1},{3,2},{4,3},{5,4},{6,5},{7,6},{8,7},{9,8},{10,9},{11,1... | collective-permute-start | bytes 245768 | tf_op jit(solution)/shard_map/ppermute | solution.py:19
  17.5 4.6 %collective-permute-start.2 = (f32[16,1,1280]{2,0,1:T(8,128)S(1)}, f32[16,1,1280]{2,0,1:T(8,128)S(1)}, u32[]{:S(2)}, u32[]{:S(2)}) collective-permute-start(f32[16,1,1280]{2,0,1:T(8,128)S(1)} %get-tuple-element.77), channel_id=1, source_target_pairs={{0,1},{1,2},{2,3},{3,4},{4,5},{5,6},{6,7},{7,8},{8,9},{9,10},{10,1... | collective-permute-start | bytes 245768 | tf_op jit(solution)/shard_map/ppermute | solution.py:16
  20.6 5.2 %collective-permute-start.3 = (f32[16,1,1280]{2,0,1:T(8,128)S(1)}, f32[16,1,1280]{2,0,1:T(8,128)S(1)}, u32[]{:S(2)}, u32[]{:S(2)}) collective-permute-start(f32[16,1,1280]{2,0,1:T(8,128)S(1)} %get-tuple-element.78), channel_id=1, source_target_pairs={{1,0},{2,1},{3,2},{4,3},{5,4},{6,5},{7,6},{8,7},{9,8},{10,9},{11,1... | collective-permute-start | bytes 245768 | tf_op jit(solution)/shard_map/ppermute | solution.py:19
  25.9 6.5 %collective-permute-start.4 = (f32[16,1,1280]{2,0,1:T(8,128)S(1)}, f32[16,1,1280]{2,0,1:T(8,128)S(1)}, u32[]{:S(2)}, u32[]{:S(2)}) collective-permute-start(f32[16,1,1280]{2,0,1:T(8,128)S(1)} %get-tuple-element.75), channel_id=1, source_target_pairs={{0,1},{1,2},{2,3},{3,4},{4,5},{5,6},{6,7},{7,8},{8,9},{9,10},{10,1... | collective-permute-start | bytes 245768 | tf_op jit(solution)/shard_map/ppermute | solution.py:16
  30.9 5.2 %collective-permute-start.5 = (f32[16,1,1280]{2,0,1:T(8,128)S(1)}, f32[16,1,1280]{2,0,1:T(8,128)S(1)}, u32[]{:S(2)}, u32[]{:S(2)}) collective-permute-start(f32[16,1,1280]{2,0,1:T(8,128)S(1)} %get-tuple-element.76), channel_id=1, source_target_pairs={{1,0},{2,1},{3,2},{4,3},{5,4},{6,5},{7,6},{8,7},{9,8},{10,9},{11,1... | collective-permute-start | bytes 245768 | tf_op jit(solution)/shard_map/ppermute | solution.py:19
  36.2 5.4 %collective-permute-start.6 = (bf16[16,1,1280]{2,0,1:T(8,128)(2,1)S(1)}, bf16[16,1,1280]{2,0,1:T(8,128)(2,1)S(1)}, u32[]{:S(2)}, u32[]{:S(2)}) collective-permute-start(bf16[16,1,1280]{2,0,1:T(8,128)(2,1)S(1)} %get-tuple-element.83), channel_id=1, source_target_pairs={{0,1},{1,2},{2,3},{3,4},{4,5},{5,6},{6,7},{7,8},{8,9},{9,10},{10,1... | collective-permute-start | bytes 122888 | tf_op jit(solution)/shard_map/ppermute | solution.py:16
  40.2 5.0 %collective-permute-start.7 = (bf16[16,1,1280]{2,0,1:T(8,128)(2,1)S(1)}, bf16[16,1,1280]{2,0,1:T(8,128)(2,1)S(1)}, u32[]{:S(2)}, u32[]{:S(2)}) collective-permute-start(bf16[16,1,1280]{2,0,1:T(8,128)(2,1)S(1)} %get-tuple-element.84), channel_id=1, source_target_pairs={{1,0},{2,1},{3,2},{4,3},{5,4},{6,5},{7,6},{8,7},{9,8},{10,9},{11,1... | collective-permute-start | bytes 122888 | tf_op jit(solution)/shard_map/ppermute | solution.py:19
  49.8 1.3 copy-start
  51.2 2.8 copy-start.3
  51.2 2.8 copy-start.4
  51.2 42.5 %copy-start.8 = (f32[16,320]{1,0:T(8,128)S(1)}, f32[16,320]{1,0:T(8,128)}, u32[]{:S(2)}) copy-start(f32[16,320]{1,0:T(8,128)} %param.18) | copy-start | bytes 61444
  54.0 51.8 %copy-start.7 = (f32[1,128,8]{1,2,0:T(8,128)S(1)}, f32[1,128,8]{1,2,0:T(8,128)}, u32[]{:S(2)}) copy-start(f32[1,128,8]{1,2,0:T(8,128)} %param.24) | copy-start | bytes 12292
  54.0 52.5 %copy-start.6 = (f32[1,128,8]{1,2,0:T(8,128)S(1)}, f32[1,128,8]{1,2,0:T(8,128)}, u32[]{:S(2)}) copy-start(f32[1,128,8]{1,2,0:T(8,128)} %param.23) | copy-start | bytes 12292
  93.6 41.5 %copy-start.5 = (s32[1,128,8]{1,2,0:T(8,128)S(1)}, s32[1,128,8]{1,2,0:T(8,128)}, u32[]{:S(2)}) copy-start(s32[1,128,8]{1,2,0:T(8,128)} %param.22) | copy-start | bytes 12292
  95.9 19.6 %all-to-all-start = ((f32[128,1,8]{2,1,0:T(1,128)}), f32[128,1,8]{2,1,0:T(1,128)S(1)}, u32[]{:S(2)}, u32[]{:S(2)}) async-start(f32[128,1,8]{2,1,0:T(1,128)} %copy.126), calls=%async_computation | async-start | bytes 131072 | tf_op jit(solution)/shard_map/all_to_all | solution.py:182
  116.5 18.4 %all-to-all-start.1 = ((f32[128,8,8]{2,1,0:T(8,128)}), f32[128,8,8]{2,1,0:T(8,128)S(1)}, u32[]{:S(2)}, u32[]{:S(2)}) async-start(f32[128,8,8]{2,1,0:T(8,128)} %bitcast.22), calls=%async_computation.1 | async-start | bytes 1048576 | tf_op jit(solution)/shard_map/all_to_all | solution.py:187
  146.7 10.6 %slice-start = ((s8[6553600]{0:T(1024)(128)(4,1)}), s8[4194304]{0:T(1024)(128)(4,1)S(1)}, s32[]{:S(2)}) async-start(s8[6553600]{0:T(1024)(128)(4,1)} %bitcast.154), calls=%async_computation.7 | async-start | bytes 8388608
  147.8 9.4 %slice-start.1 = ((s8[6553600]{0:T(1024)(128)(4,1)}), s8[2359296]{0:T(1024)(128)(4,1)S(1)}, s32[]{:S(2)}) async-start(s8[6553600]{0:T(1024)(128)(4,1)} %bitcast.154), calls=%async_computation.8 | async-start | bytes 4718592
  147.9 5.4 %collective-permute-start.8 = (f32[16,1,2560]{2,0,1:T(8,128)S(1)}, f32[16,1,2560]{2,0,1:T(8,128)S(1)}, u32[]{:S(2)}, u32[]{:S(2)}) collective-permute-start(f32[16,1,2560]{2,0,1:T(8,128)S(1)} %get-tuple-element.54), channel_id=1, source_target_pairs={{0,1},{1,2},{2,3},{3,4},{4,5},{5,6},{6,7},{7,8},{8,9},{9,10},{10,1... | collective-permute-start | bytes 491528 | tf_op jit(solution)/shard_map/ppermute | solution.py:16
  150.4 6.8 %collective-permute-start.9 = (f32[16,1,2560]{2,0,1:T(8,128)S(1)}, f32[16,1,2560]{2,0,1:T(8,128)S(1)}, u32[]{:S(2)}, u32[]{:S(2)}) collective-permute-start(f32[16,1,2560]{2,0,1:T(8,128)S(1)} %get-tuple-element.53), channel_id=1, source_target_pairs={{1,0},{2,1},{3,2},{4,3},{5,4},{6,5},{7,6},{8,7},{9,8},{10,9},{11,1... | collective-permute-start | bytes 491528 | tf_op jit(solution)/shard_map/ppermute | solution.py:19
  159.4 26.6 %copy-start.1 = (f32[16,4,1280]{2,1,0:T(4,128)S(1)}, f32[16,4,1280]{2,1,0:T(4,128)}, u32[]{:S(2)}) copy-start(f32[16,4,1280]{2,1,0:T(4,128)} %param.16) | copy-start | bytes 983044
  159.4 4.1 %collective-permute-start.10 = (f32[16,1,1280]{2,0,1:T(8,128)S(1)}, f32[16,1,1280]{2,0,1:T(8,128)S(1)}, u32[]{:S(2)}, u32[]{:S(2)}) collective-permute-start(f32[16,1,1280]{2,0,1:T(8,128)S(1)} %get-tuple-element.73), channel_id=1, source_target_pairs={{0,1},{1,2},{2,3},{3,4},{4,5},{5,6},{6,7},{7,8},{8,9},{9,10},{10,1... | collective-permute-start | bytes 245768 | tf_op jit(solution)/shard_map/ppermute | solution.py:16
  162.0 5.2 %collective-permute-start.11 = (f32[16,1,1280]{2,0,1:T(8,128)S(1)}, f32[16,1,1280]{2,0,1:T(8,128)S(1)}, u32[]{:S(2)}, u32[]{:S(2)}) collective-permute-start(f32[16,1,1280]{2,0,1:T(8,128)S(1)} %get-tuple-element.74), channel_id=1, source_target_pairs={{1,0},{2,1},{3,2},{4,3},{5,4},{6,5},{7,6},{8,7},{9,8},{10,9},{11,1... | collective-permute-start | bytes 245768 | tf_op jit(solution)/shard_map/ppermute | solution.py:19
  167.3 5.4 %collective-permute-start.12 = (f32[16,1,1280]{2,0,1:T(8,128)S(1)}, f32[16,1,1280]{2,0,1:T(8,128)S(1)}, u32[]{:S(2)}, u32[]{:S(2)}) collective-permute-start(f32[16,1,1280]{2,0,1:T(8,128)S(1)} %get-tuple-element.71), channel_id=1, source_target_pairs={{0,1},{1,2},{2,3},{3,4},{4,5},{5,6},{6,7},{7,8},{8,9},{9,10},{10,1... | collective-permute-start | bytes 245768 | tf_op jit(solution)/shard_map/ppermute | solution.py:16
  171.2 5.2 %collective-permute-start.13 = (f32[16,1,1280]{2,0,1:T(8,128)S(1)}, f32[16,1,1280]{2,0,1:T(8,128)S(1)}, u32[]{:S(2)}, u32[]{:S(2)}) collective-permute-start(f32[16,1,1280]{2,0,1:T(8,128)S(1)} %get-tuple-element.72), channel_id=1, source_target_pairs={{1,0},{2,1},{3,2},{4,3},{5,4},{6,5},{7,6},{8,7},{9,8},{10,9},{11,1... | collective-permute-start | bytes 245768 | tf_op jit(solution)/shard_map/ppermute | solution.py:19
  176.5 5.8 %collective-permute-start.14 = (f32[16,1,1280]{2,0,1:T(8,128)S(1)}, f32[16,1,1280]{2,0,1:T(8,128)S(1)}, u32[]{:S(2)}, u32[]{:S(2)}) collective-permute-start(f32[16,1,1280]{2,0,1:T(8,128)S(1)} %get-tuple-element.69), channel_id=1, source_target_pairs={{0,1},{1,2},{2,3},{3,4},{4,5},{5,6},{6,7},{7,8},{8,9},{9,10},{10,1... | collective-permute-start | bytes 245768 | tf_op jit(solution)/shard_map/ppermute | solution.py:16
  180.8 5.2 %collective-permute-start.15 = (f32[16,1,1280]{2,0,1:T(8,128)S(1)}, f32[16,1,1280]{2,0,1:T(8,128)S(1)}, u32[]{:S(2)}, u32[]{:S(2)}) collective-permute-start(f32[16,1,1280]{2,0,1:T(8,128)S(1)} %get-tuple-element.70), channel_id=1, source_target_pairs={{1,0},{2,1},{3,2},{4,3},{5,4},{6,5},{7,6},{8,7},{9,8},{10,9},{11,1... | collective-permute-start | bytes 245768 | tf_op jit(solution)/shard_map/ppermute | solution.py:19
  186.7 5.2 %collective-permute-start.16 = (f32[16,1,1280]{2,0,1:T(8,128)S(1)}, f32[16,1,1280]{2,0,1:T(8,128)S(1)}, u32[]{:S(2)}, u32[]{:S(2)}) collective-permute-start(f32[16,1,1280]{2,0,1:T(8,128)S(1)} %get-tuple-element.67), channel_id=1, source_target_pairs={{0,1},{1,2},{2,3},{3,4},{4,5},{5,6},{6,7},{7,8},{8,9},{9,10},{10,1... | collective-permute-start | bytes 245768 | tf_op jit(solution)/shard_map/ppermute | solution.py:16
  190.5 5.2 %collective-permute-start.17 = (f32[16,1,1280]{2,0,1:T(8,128)S(1)}, f32[16,1,1280]{2,0,1:T(8,128)S(1)}, u32[]{:S(2)}, u32[]{:S(2)}) collective-permute-start(f32[16,1,1280]{2,0,1:T(8,128)S(1)} %get-tuple-element.68), channel_id=1, source_target_pairs={{1,0},{2,1},{3,2},{4,3},{5,4},{6,5},{7,6},{8,7},{9,8},{10,9},{11,1... | collective-permute-start | bytes 245768 | tf_op jit(solution)/shard_map/ppermute | solution.py:19
  195.7 5.5 %collective-permute-start.18 = (f32[16,1,1280]{2,0,1:T(8,128)S(1)}, f32[16,1,1280]{2,0,1:T(8,128)S(1)}, u32[]{:S(2)}, u32[]{:S(2)}) collective-permute-start(f32[16,1,1280]{2,0,1:T(8,128)S(1)} %get-tuple-element.65), channel_id=1, source_target_pairs={{0,1},{1,2},{2,3},{3,4},{4,5},{5,6},{6,7},{7,8},{8,9},{9,10},{10,1... | collective-permute-start | bytes 245768 | tf_op jit(solution)/shard_map/ppermute | solution.py:16
  199.8 5.2 %collective-permute-start.19 = (f32[16,1,1280]{2,0,1:T(8,128)S(1)}, f32[16,1,1280]{2,0,1:T(8,128)S(1)}, u32[]{:S(2)}, u32[]{:S(2)}) collective-permute-start(f32[16,1,1280]{2,0,1:T(8,128)S(1)} %get-tuple-element.66), channel_id=1, source_target_pairs={{1,0},{2,1},{3,2},{4,3},{5,4},{6,5},{7,6},{8,7},{9,8},{10,9},{11,1... | collective-permute-start | bytes 245768 | tf_op jit(solution)/shard_map/ppermute | solution.py:19
  205.0 5.5 %collective-permute-start.20 = (f32[16,1,1280]{2,0,1:T(8,128)S(1)}, f32[16,1,1280]{2,0,1:T(8,128)S(1)}, u32[]{:S(2)}, u32[]{:S(2)}) collective-permute-start(f32[16,1,1280]{2,0,1:T(8,128)S(1)} %get-tuple-element.63), channel_id=1, source_target_pairs={{0,1},{1,2},{2,3},{3,4},{4,5},{5,6},{6,7},{7,8},{8,9},{9,10},{10,1... | collective-permute-start | bytes 245768 | tf_op jit(solution)/shard_map/ppermute | solution.py:16
  209.1 5.2 %collective-permute-start.21 = (f32[16,1,1280]{2,0,1:T(8,128)S(1)}, f32[16,1,1280]{2,0,1:T(8,128)S(1)}, u32[]{:S(2)}, u32[]{:S(2)}) collective-permute-start(f32[16,1,1280]{2,0,1:T(8,128)S(1)} %get-tuple-element.64), channel_id=1, source_target_pairs={{1,0},{2,1},{3,2},{4,3},{5,4},{6,5},{7,6},{8,7},{9,8},{10,9},{11,1... | collective-permute-start | bytes 245768 | tf_op jit(solution)/shard_map/ppermute | solution.py:19
  214.3 24.6 %collective-permute-start.22 = (bf16[16,1,1280]{2,0,1:T(8,128)(2,1)S(1)}, bf16[16,1,1280]{2,0,1:T(8,128)(2,1)S(1)}, u32[]{:S(2)}, u32[]{:S(2)}) collective-permute-start(bf16[16,1,1280]{2,0,1:T(8,128)(2,1)S(1)} %get-tuple-element.81), channel_id=1, source_target_pairs={{0,1},{1,2},{2,3},{3,4},{4,5},{5,6},{6,7},{7,8},{8,9},{9,10},{10,1... | collective-permute-start | bytes 122888 | tf_op jit(solution)/shard_map/ppermute | solution.py:16
  218.4 20.5 %collective-permute-start.23 = (bf16[16,1,1280]{2,0,1:T(8,128)(2,1)S(1)}, bf16[16,1,1280]{2,0,1:T(8,128)(2,1)S(1)}, u32[]{:S(2)}, u32[]{:S(2)}) collective-permute-start(bf16[16,1,1280]{2,0,1:T(8,128)(2,1)S(1)} %get-tuple-element.82), channel_id=1, source_target_pairs={{1,0},{2,1},{3,2},{4,3},{5,4},{6,5},{7,6},{8,7},{9,8},{10,9},{11,1... | collective-permute-start | bytes 122888 | tf_op jit(solution)/shard_map/ppermute | solution.py:19
  220.6 32.3 %all-to-all-start.2 = ((f32[128,8,8]{2,1,0:T(8,128)}), f32[128,8,8]{2,1,0:T(8,128)S(1)}, u32[]{:S(2)}, u32[]{:S(2)}) async-start(f32[128,8,8]{2,1,0:T(8,128)} %bitcast.31), calls=%async_computation.2 | async-start | bytes 1048576 | tf_op jit(solution)/shard_map/all_to_all | solution.py:190
  238.8 39.2 %reduce-scatter.9.cloned.1.call-start = ((), (), s32[]{:S(2)}) async-start(), calls=%async_computation.6 | async-start | bytes 1474560
Sparse Core Ops, SparseCore 0:
  54.1 38.4 reduce-scatter.6
  246.7 31.3 reduce-scatter.8
where the time goes:
time: 361 us; the launch traced here: 360 us
  waiting for transfers between devices  137 us (38%)
  starting transfers between devices  93.4 us (26%)
  blocking collectives  67.6 us (19%)
  matrix products  25.3 us (7%)
  between operations  17.3 us (5%)
  local copies, waits for them, and re-layouts  12 us (3%)
  other arithmetic  7.7 us (2%)
    psum x1, blocking collectives, global_sum(): return lax.psum(values, ('member', 'tile'))  67.6 us
    unnamed x4, waiting for transfers between devices  63.6 us
    ppermute x12, starting transfers between devices, padded_2(): lax.ppermute(lax.slice_in_dim(block, block.shape[dim] - width, None, axis...  45.2 us
    ppermute x12, waiting for transfers between devices, padded_2(): lax.ppermute(lax.slice_in_dim(block, 0, width, axis=dim), axis, backward)  41.1 us
    all_to_all x1, starting transfers between devices, shards(): lax.all_to_all(fan_out(obs_weight), ('member', 'tile'), split_axis=0, con...  18.2 us
    ppermute x12, starting transfers between devices, padded_2(): lax.ppermute(lax.slice_in_dim(block, 0, width, axis=dim), axis, backward)  15.7 us
    all_to_all x1, waiting for transfers between devices, shards(): lax.all_to_all(fan_out(residual), ('member', 'tile'), split_axis=0, conca...  14.1 us
    dot_general x1, matrix products, spread_tile(): jnp.einsum('bmsr,bmsc->rmc', weighted, column_factor, precision=lax.Preci...  11.3 us
  transfers between devices with their start and end apart: 29, of which 26 were waited for; matrix products, arithmetic and copies ran while one was open for 3% of the time, Pallas kernels for 0%

commit v1 on v0

--- a/solution.py
+++ b/solution.py
@@ -141,7 +141,7 @@
 
 
 def global_sum(values):
-    return lax.psum(values, ("member", "tile"))
+    return jax.lax.psum(jax.lax.psum(values, "member"), "tile")
 
 
 def shards(

time: 361 us -> 350 us (0.970)
  the two profiles are of different devices: /device:TPU:1 before, /device:TPU:0 now
where the time goes in v1:
time: 350 us; the launch traced here: 349 us
  waiting for transfers between devices  149 us (43%)
  starting transfers between devices  83.7 us (24%)
  blocking collectives  54.6 us (16%)
  matrix products  25.3 us (7%)
  between operations  17.3 us (5%)
  local copies, waits for them, and re-layouts  12 us (3%)
  other arithmetic  7.7 us (2%)
    unnamed x4, waiting for transfers between devices  64.4 us
    psum x2, blocking collectives, global_sum(): return jax.lax.psum(jax.lax.psum(values, 'member'), 'tile')  54.6 us
    ppermute x12, waiting for transfers between devices, padded_2(): lax.ppermute(lax.slice_in_dim(block, 0, width, axis=dim), axis, backward)  47.2 us
    ppermute x12, starting transfers between devices, padded_2(): lax.ppermute(lax.slice_in_dim(block, block.shape[dim] - width, None, axis...  46.7 us
    ppermute x12, starting transfers between devices, padded_2(): lax.ppermute(lax.slice_in_dim(block, 0, width, axis=dim), axis, backward)  15.7 us
    all_to_all x1, waiting for transfers between devices, shards(): lax.all_to_all(fan_out(residual), ('member', 'tile'), split_axis=0, conca...  13.4 us
    dot_general x1, matrix products, spread_tile(): jnp.einsum('bmsr,bmsc->rmc', weighted, column_factor, precision=lax.Preci...  11.3 us
    ppermute x12, waiting for transfers between devices, padded_2(): lax.ppermute(lax.slice_in_dim(block, block.shape[dim] - width, None, axis...  9.15 us
  transfers between devices with their start and end apart: 29, of which 27 were waited for; matrix products, arithmetic and copies ran while one was open for 3% of the time, Pallas kernels for 0%

profile of v1, /device:TPU:0, one launch (start us, length us, event | category | flops | bytes accessed | tf_op | source)
XLA Modules:
  0.0 349.2 jit_solution(3955521573306211919)
XLA Ops:
  7.2 1.0 copy.144
  8.3 3.5 %collective-permute-start = (f32[16,1,1280]{2,0,1:T(8,128)S(1)}, f32[16,1,1280]{2,0,1:T(8,128)S(1)}, u32[]{:S(2)}, u32[]{:S(2)}) collective-permute-start(f32[16,1,1280]{2,0,1:T(8,128)S(1)} %get-tuple-element.81), channel_id=1, source_target_pairs={{0,1},{1,2},{2,3},{3,4},{4,5},{5,6},{6,7},{7,8},{8,9},{9,10},{10,1... | collective-permute-start | bytes 245768 | tf_op jit(solution)/shard_map/ppermute | solution.py:16
  11.8 1.3 collective-permute-start.1
  13.8 4.3 %collective-permute-done.1 = f32[16,1,1280]{2,0,1:T(8,128)S(1)} collective-permute-done((f32[16,1,1280]{2,0,1:T(8,128)S(1)}, f32[16,1,1280]{2,0,1:T(8,128)S(1)}, u32[]{:S(2)}, u32[]{:S(2)}) %collective-permute-start.1) | collective-permute-done | bytes 81952 | tf_op jit(solution)/shard_map/ppermute | solution.py:19
  18.2 3.4 collective-permute-start.2
  21.6 1.3 collective-permute-start.3
  23.7 4.3 %collective-permute-done.3 = f32[16,1,1280]{2,0,1:T(8,128)S(1)} collective-permute-done((f32[16,1,1280]{2,0,1:T(8,128)S(1)}, f32[16,1,1280]{2,0,1:T(8,128)S(1)}, u32[]{:S(2)}, u32[]{:S(2)}) %collective-permute-start.3) | collective-permute-done | bytes 81952 | tf_op jit(solution)/shard_map/ppermute | solution.py:19
  28.0 5.0 %collective-permute-start.4 = (f32[16,1,1280]{2,0,1:T(8,128)S(1)}, f32[16,1,1280]{2,0,1:T(8,128)S(1)}, u32[]{:S(2)}, u32[]{:S(2)}) collective-permute-start(f32[16,1,1280]{2,0,1:T(8,128)S(1)} %get-tuple-element.77), channel_id=1, source_target_pairs={{0,1},{1,2},{2,3},{3,4},{4,5},{5,6},{6,7},{7,8},{8,9},{9,10},{10,1... | collective-permute-start | bytes 245768 | tf_op jit(solution)/shard_map/ppermute | solution.py:16
  33.1 1.3 collective-permute-start.5
  35.1 4.3 %collective-permute-done.5 = f32[16,1,1280]{2,0,1:T(8,128)S(1)} collective-permute-done((f32[16,1,1280]{2,0,1:T(8,128)S(1)}, f32[16,1,1280]{2,0,1:T(8,128)S(1)}, u32[]{:S(2)}, u32[]{:S(2)}) %collective-permute-start.5) | collective-permute-done | bytes 81952 | tf_op jit(solution)/shard_map/ppermute | solution.py:19
  39.5 4.0 %collective-permute-start.6 = (bf16[16,1,1280]{2,0,1:T(8,128)(2,1)S(1)}, bf16[16,1,1280]{2,0,1:T(8,128)(2,1)S(1)}, u32[]{:S(2)}, u32[]{:S(2)}) collective-permute-start(bf16[16,1,1280]{2,0,1:T(8,128)(2,1)S(1)} %get-tuple-element.85), channel_id=1, source_target_pairs={{0,1},{1,2},{2,3},{3,4},{4,5},{5,6},{6,7},{7,8},{8,9},{9,10},{10,1... | collective-permute-start | bytes 122888 | tf_op jit(solution)/shard_map/ppermute | solution.py:16
  43.5 1.3 collective-permute-start.7
  45.2 4.2 %collective-permute-done.7 = bf16[16,1,1280]{2,0,1:T(8,128)(2,1)S(1)} collective-permute-done((bf16[16,1,1280]{2,0,1:T(8,128)(2,1)S(1)}, bf16[16,1,1280]{2,0,1:T(8,128)(2,1)S(1)}, u32[]{:S(2)}, u32[]{:S(2)}) %collective-permute-start.7) | collective-permute-done | bytes 40992 | tf_op jit(solution)/shard_map/ppermute | solution.py:19
  49.4 4.0 %fusion.8 = f32[16,6,2560]{2,0,1:T(8,128)S(1)} fusion(bf16[1280,2560]{1,0:T(8,128)(2,1)} %param.17, bf16[16,1,1280]{2,0,1:T(8,128)(2,1)S(1)} %collective-permute-done.7, bf16[16,4,1280]{2,0,1:T(8,128)(2,1)S(1)} %fusion.56, bf16[16,1,1280]{2,0,1:T(8,128)(2,1)S(1)} %collective-permute-done.6), kind=kOutput, calls=%fused_computation.10 | convolution fusion | flops 629391360 | bytes 7782400 | tf_op jit(solution)/shard_map/dot_general | solution.py:79
  54.3 1.1 copy-done
  55.4 1.3 fusion.15
  56.7 1.5 copy.150
  58.3 36.4 %reduce-scatter.7.cloned.1.call-done = f32[320,16]{1,0:T(8,128)} async-done(((f32[2560,16]{1,0:T(8,128)}), f32[320,16]{1,0:T(8,128)}) %reduce-scatter.7.cloned.1.call-update) | async-done | bytes 20496
  94.7 1.0 copy.151
  95.7 1.5 fusion.17
  97.9 7.5 %all-to-all-start = ((f32[128,1,8]{2,1,0:T(1,128)}), f32[128,1,8]{2,1,0:T(1,128)S(1)}, u32[]{:S(2)}, u32[]{:S(2)}) async-start(f32[128,1,8]{2,1,0:T(1,128)} %copy.126), calls=%async_computation | async-start | bytes 131072 | tf_op jit(solution)/shard_map/all_to_all | solution.py:182
  106.2 8.6 %all-to-all-done = f32[128,1,8]{2,1,0:T(1,128)S(1)} async-done(((f32[128,1,8]{2,1,0:T(1,128)}), f32[128,1,8]{2,1,0:T(1,128)S(1)}, u32[]{:S(2)}, u32[]{:S(2)}) %all-to-all-start) | async-done | bytes 4128 | tf_op jit(solution)/shard_map/all_to_all | solution.py:182
  115.9 4.8 %all-to-all-start.1 = ((f32[128,8,8]{2,1,0:T(8,128)}), f32[128,8,8]{2,1,0:T(8,128)S(1)}, u32[]{:S(2)}, u32[]{:S(2)}) async-start(f32[128,8,8]{2,1,0:T(8,128)} %bitcast.22), calls=%async_computation.1 | async-start | bytes 1048576 | tf_op jit(solution)/shard_map/all_to_all | solution.py:187
  120.7 13.4 %all-to-all-done.1 = f32[128,8,8]{2,1,0:T(8,128)S(1)} async-done(((f32[128,8,8]{2,1,0:T(8,128)}), f32[128,8,8]{2,1,0:T(8,128)S(1)}, u32[]{:S(2)}, u32[]{:S(2)}) %all-to-all-start.1) | async-done | bytes 32800 | tf_op jit(solution)/shard_map/all_to_all | solution.py:187
  134.3 11.3 %fusion.19 = f32[16,8,320]{2,0,1:T(8,128)S(1)} fusion(f32[128,8,8]{0,2,1:T(8,128)S(1)} %bitcast.162, s32[128,8,8]{0,2,1:T(8,128)S(1)} %get-tuple-element.91, f32[128,8,8]{0,2,1:T(8,128)S(1)} %get-tuple-element.98, s32[128,8,8]{0,2,1:T(8,128)S(1)} %get-tuple-element.92, f32[128,8,8]{0,2,1:T(8,128)S(1)} %broadcast_select_fusion, ...), kind=kOutput, calls=%fused_computation.31 | convolution fusion | flops 517210112 | bytes 458752 | tf_op jit(solution)/shard_map/bmsr,bmsc->rmc/dot_general | solution.py:131
  145.8 0.8 convert_multiply_fusion.1
  147.0 2.7 collective-permute-start.8
  149.8 1.5 collective-permute-start.9
  151.4 1.9 collective-permute-done.8
  153.3 4.2 %collective-permute-done.9 = f32[16,1,2560]{2,0,1:T(8,128)S(1)} collective-permute-done((f32[16,1,2560]{2,0,1:T(8,128)S(1)}, f32[16,1,2560]{2,0,1:T(8,128)S(1)}, u32[]{:S(2)}, u32[]{:S(2)}) %collective-permute-start.9) | collective-permute-done | bytes 163872 | tf_op jit(solution)/shard_map/ppermute | solution.py:19
  157.6 2.1 fusion.6
  159.7 2.5 collective-permute-start.10
  162.2 1.3 collective-permute-start.11
  164.2 4.3 %collective-permute-done.11 = f32[16,1,1280]{2,0,1:T(8,128)S(1)} collective-permute-done((f32[16,1,1280]{2,0,1:T(8,128)S(1)}, f32[16,1,1280]{2,0,1:T(8,128)S(1)}, u32[]{:S(2)}, u32[]{:S(2)}) %collective-permute-start.11) | collective-permute-done | bytes 81952 | tf_op jit(solution)/shard_map/ppermute | solution.py:19
  168.6 5.4 %collective-permute-start.12 = (f32[16,1,1280]{2,0,1:T(8,128)S(1)}, f32[16,1,1280]{2,0,1:T(8,128)S(1)}, u32[]{:S(2)}, u32[]{:S(2)}) collective-permute-start(f32[16,1,1280]{2,0,1:T(8,128)S(1)} %get-tuple-element.73), channel_id=1, source_target_pairs={{0,1},{1,2},{2,3},{3,4},{4,5},{5,6},{6,7},{7,8},{8,9},{9,10},{10,1... | collective-permute-start | bytes 245768 | tf_op jit(solution)/shard_map/ppermute | solution.py:16
  174.0 1.3 collective-permute-start.13
  176.0 4.3 %collective-permute-done.13 = f32[16,1,1280]{2,0,1:T(8,128)S(1)} collective-permute-done((f32[16,1,1280]{2,0,1:T(8,128)S(1)}, f32[16,1,1280]{2,0,1:T(8,128)S(1)}, u32[]{:S(2)}, u32[]{:S(2)}) %collective-permute-start.13) | collective-permute-done | bytes 81952 | tf_op jit(solution)/shard_map/ppermute | solution.py:19
  180.4 4.0 %collective-permute-start.14 = (f32[16,1,1280]{2,0,1:T(8,128)S(1)}, f32[16,1,1280]{2,0,1:T(8,128)S(1)}, u32[]{:S(2)}, u32[]{:S(2)}) collective-permute-start(f32[16,1,1280]{2,0,1:T(8,128)S(1)} %get-tuple-element.71), channel_id=1, source_target_pairs={{0,1},{1,2},{2,3},{3,4},{4,5},{5,6},{6,7},{7,8},{8,9},{9,10},{10,1... | collective-permute-start | bytes 245768 | tf_op jit(solution)/shard_map/ppermute | solution.py:16
  184.5 1.3 collective-permute-start.15
  186.5 4.3 %collective-permute-done.15 = f32[16,1,1280]{2,0,1:T(8,128)S(1)} collective-permute-done((f32[16,1,1280]{2,0,1:T(8,128)S(1)}, f32[16,1,1280]{2,0,1:T(8,128)S(1)}, u32[]{:S(2)}, u32[]{:S(2)}) %collective-permute-start.15) | collective-permute-done | bytes 81952 | tf_op jit(solution)/shard_map/ppermute | solution.py:19
  191.5 4.0 %collective-permute-start.16 = (f32[16,1,1280]{2,0,1:T(8,128)S(1)}, f32[16,1,1280]{2,0,1:T(8,128)S(1)}, u32[]{:S(2)}, u32[]{:S(2)}) collective-permute-start(f32[16,1,1280]{2,0,1:T(8,128)S(1)} %get-tuple-element.69), channel_id=1, source_target_pairs={{0,1},{1,2},{2,3},{3,4},{4,5},{5,6},{6,7},{7,8},{8,9},{9,10},{10,1... | collective-permute-start | bytes 245768 | tf_op jit(solution)/shard_map/ppermute | solution.py:16
  195.6 1.3 collective-permute-start.17
  197.6 4.3 %collective-permute-done.17 = f32[16,1,1280]{2,0,1:T(8,128)S(1)} collective-permute-done((f32[16,1,1280]{2,0,1:T(8,128)S(1)}, f32[16,1,1280]{2,0,1:T(8,128)S(1)}, u32[]{:S(2)}, u32[]{:S(2)}) %collective-permute-start.17) | collective-permute-done | bytes 81952 | tf_op jit(solution)/shard_map/ppermute | solution.py:19
  202.0 4.0 %collective-permute-start.18 = (f32[16,1,1280]{2,0,1:T(8,128)S(1)}, f32[16,1,1280]{2,0,1:T(8,128)S(1)}, u32[]{:S(2)}, u32[]{:S(2)}) collective-permute-start(f32[16,1,1280]{2,0,1:T(8,128)S(1)} %get-tuple-element.67), channel_id=1, source_target_pairs={{0,1},{1,2},{2,3},{3,4},{4,5},{5,6},{6,7},{7,8},{8,9},{9,10},{10,1... | collective-permute-start | bytes 245768 | tf_op jit(solution)/shard_map/ppermute | solution.py:16
  206.0 1.3 collective-permute-start.19
  208.0 4.3 %collective-permute-done.19 = f32[16,1,1280]{2,0,1:T(8,128)S(1)} collective-permute-done((f32[16,1,1280]{2,0,1:T(8,128)S(1)}, f32[16,1,1280]{2,0,1:T(8,128)S(1)}, u32[]{:S(2)}, u32[]{:S(2)}) %collective-permute-start.19) | collective-permute-done | bytes 81952 | tf_op jit(solution)/shard_map/ppermute | solution.py:19
  212.4 4.0 %collective-permute-start.20 = (f32[16,1,1280]{2,0,1:T(8,128)S(1)}, f32[16,1,1280]{2,0,1:T(8,128)S(1)}, u32[]{:S(2)}, u32[]{:S(2)}) collective-permute-start(f32[16,1,1280]{2,0,1:T(8,128)S(1)} %get-tuple-element.65), channel_id=1, source_target_pairs={{0,1},{1,2},{2,3},{3,4},{4,5},{5,6},{6,7},{7,8},{8,9},{9,10},{10,1... | collective-permute-start | bytes 245768 | tf_op jit(solution)/shard_map/ppermute | solution.py:16
  216.5 1.3 collective-permute-start.21
  217.8 1.1 collective-permute-done.20
  218.8 4.4 %collective-permute-done.21 = f32[16,1,1280]{2,0,1:T(8,128)S(1)} collective-permute-done((f32[16,1,1280]{2,0,1:T(8,128)S(1)}, f32[16,1,1280]{2,0,1:T(8,128)S(1)}, u32[]{:S(2)}, u32[]{:S(2)}) %collective-permute-start.21) | collective-permute-done | bytes 81952 | tf_op jit(solution)/shard_map/ppermute | solution.py:19
  223.3 4.0 %collective-permute-start.22 = (bf16[16,1,1280]{2,0,1:T(8,128)(2,1)S(1)}, bf16[16,1,1280]{2,0,1:T(8,128)(2,1)S(1)}, u32[]{:S(2)}, u32[]{:S(2)}) collective-permute-start(bf16[16,1,1280]{2,0,1:T(8,128)(2,1)S(1)} %get-tuple-element.83), channel_id=1, source_target_pairs={{0,1},{1,2},{2,3},{3,4},{4,5},{5,6},{6,7},{7,8},{8,9},{9,10},{10,1... | collective-permute-start | bytes 122888 | tf_op jit(solution)/shard_map/ppermute | solution.py:16
  227.4 1.3 collective-permute-start.23
  228.8 0.8 broadcast_in_dim.138
  229.6 8.9 %all-to-all-start.2 = ((f32[128,8,8]{2,1,0:T(8,128)}), f32[128,8,8]{2,1,0:T(8,128)S(1)}, u32[]{:S(2)}, u32[]{:S(2)}) async-start(f32[128,8,8]{2,1,0:T(8,128)} %bitcast.31), calls=%async_computation.2 | async-start | bytes 1048576 | tf_op jit(solution)/shard_map/all_to_all | solution.py:190
  238.6 4.0 %fusion.4 = f32[16,6,2560]{2,0,1:T(8,128)S(1)} fusion(bf16[1280,2560]{1,0:T(8,128)(2,1)} %param.17, bf16[16,1,1280]{2,0,1:T(8,128)(2,1)S(1)} %collective-permute-done.23, bf16[16,4,1280]{2,0,1:T(8,128)(2,1)S(1)} %fusion.30, bf16[16,1,1280]{2,0,1:T(8,128)(2,1)S(1)} %collective-permute-done.22), kind=kOutput, calls=%fused_computation.6 | convolution fusion | flops 629391360 | bytes 7782400 | tf_op jit(solution)/shard_map/dot_general | solution.py:79
  243.5 1.3 fusion.16
  244.8 1.5 copy.152
  246.3 5.8 %all-to-all-done.2 = f32[128,8,8]{2,1,0:T(8,128)S(1)} async-done(((f32[128,8,8]{2,1,0:T(8,128)}), f32[128,8,8]{2,1,0:T(8,128)S(1)}, u32[]{:S(2)}, u32[]{:S(2)}) %all-to-all-start.2) | async-done | bytes 32800 | tf_op jit(solution)/shard_map/all_to_all | solution.py:190
  252.2 28.0 %reduce-scatter.9.cloned.1.call-done = f32[320,16]{1,0:T(8,128)} async-done(((f32[2560,16]{1,0:T(8,128)}), f32[320,16]{1,0:T(8,128)}) %reduce-scatter.9.cloned.1.call-update) | async-done | bytes 20496
  280.2 1.0 copy.153
  281.2 2.4 fusion.18
  284.2 13.4 %all-reduce.4 = (f32[]{:T(128)}, f32[]{:T(128)}) all-reduce(f32[]{:T(128)} %get-tuple-element.42, f32[]{:T(128)} %fusion.103), channel_id=1, replica_groups=mesh['member'=8,'tile'=16] {'member'}, use_global_device_ids=true, to_apply=%region_4.5 | all-reduce | flops 2 | bytes 16 | tf_op jit(solution)/shard_map/psum | solution.py:144
  297.5 41.3 %all-reduce.3 = (f32[]{:T(128)}, f32[]{:T(128)}) all-reduce(f32[]{:T(128)} %get-tuple-element.40, f32[]{:T(128)} %get-tuple-element.41), channel_id=1, replica_groups=mesh['member'=8,'tile'=16] {'tile'}, use_global_device_ids=true, to_apply=%region_5.6 | all-reduce | flops 2 | bytes 16 | tf_op jit(solution)/shard_map/psum | solution.py:144
  341.5 0.9 copy.145
  (92 shorter events, 13.7 us)
Async XLA Ops:
  7.2 37.7 %copy-start.2 = (s32[1,128,8,8]{1,3,2,0:T(8,128)S(1)}, s32[1,128,8,8]{1,3,2,0:T(8,128)}, u32[]{:S(2)}) copy-start(s32[1,128,8,8]{1,3,2,0:T(8,128)} %param.19) | copy-start | bytes 98308
  7.2 87.5 %reduce-scatter.7.cloned.1.call-start = ((), (), s32[]{:S(2)}) async-start(), calls=%async_computation.5 | async-start | bytes 1474560
  8.3 5.6 %collective-permute-start = (f32[16,1,1280]{2,0,1:T(8,128)S(1)}, f32[16,1,1280]{2,0,1:T(8,128)S(1)}, u32[]{:S(2)}, u32[]{:S(2)}) collective-permute-start(f32[16,1,1280]{2,0,1:T(8,128)S(1)} %get-tuple-element.81), channel_id=1, source_target_pairs={{0,1},{1,2},{2,3},{3,4},{4,5},{5,6},{6,7},{7,8},{8,9},{9,10},{10,1... | collective-permute-start | bytes 245768 | tf_op jit(solution)/shard_map/ppermute | solution.py:16
  11.8 6.3 %collective-permute-start.1 = (f32[16,1,1280]{2,0,1:T(8,128)S(1)}, f32[16,1,1280]{2,0,1:T(8,128)S(1)}, u32[]{:S(2)}, u32[]{:S(2)}) collective-permute-start(f32[16,1,1280]{2,0,1:T(8,128)S(1)} %get-tuple-element.82), channel_id=1, source_target_pairs={{1,0},{2,1},{3,2},{4,3},{5,4},{6,5},{7,6},{8,7},{9,8},{10,9},{11,1... | collective-permute-start | bytes 245768 | tf_op jit(solution)/shard_map/ppermute | solution.py:19
  18.2 5.4 %collective-permute-start.2 = (f32[16,1,1280]{2,0,1:T(8,128)S(1)}, f32[16,1,1280]{2,0,1:T(8,128)S(1)}, u32[]{:S(2)}, u32[]{:S(2)}) collective-permute-start(f32[16,1,1280]{2,0,1:T(8,128)S(1)} %get-tuple-element.79), channel_id=1, source_target_pairs={{0,1},{1,2},{2,3},{3,4},{4,5},{5,6},{6,7},{7,8},{8,9},{9,10},{10,1... | collective-permute-start | bytes 245768 | tf_op jit(solution)/shard_map/ppermute | solution.py:16
  21.6 6.3 %collective-permute-start.3 = (f32[16,1,1280]{2,0,1:T(8,128)S(1)}, f32[16,1,1280]{2,0,1:T(8,128)S(1)}, u32[]{:S(2)}, u32[]{:S(2)}) collective-permute-start(f32[16,1,1280]{2,0,1:T(8,128)S(1)} %get-tuple-element.80), channel_id=1, source_target_pairs={{1,0},{2,1},{3,2},{4,3},{5,4},{6,5},{7,6},{8,7},{9,8},{10,9},{11,1... | collective-permute-start | bytes 245768 | tf_op jit(solution)/shard_map/ppermute | solution.py:19
  28.0 7.1 %collective-permute-start.4 = (f32[16,1,1280]{2,0,1:T(8,128)S(1)}, f32[16,1,1280]{2,0,1:T(8,128)S(1)}, u32[]{:S(2)}, u32[]{:S(2)}) collective-permute-start(f32[16,1,1280]{2,0,1:T(8,128)S(1)} %get-tuple-element.77), channel_id=1, source_target_pairs={{0,1},{1,2},{2,3},{3,4},{4,5},{5,6},{6,7},{7,8},{8,9},{9,10},{10,1... | collective-permute-start | bytes 245768 | tf_op jit(solution)/shard_map/ppermute | solution.py:16
  33.1 6.3 %collective-permute-start.5 = (f32[16,1,1280]{2,0,1:T(8,128)S(1)}, f32[16,1,1280]{2,0,1:T(8,128)S(1)}, u32[]{:S(2)}, u32[]{:S(2)}) collective-permute-start(f32[16,1,1280]{2,0,1:T(8,128)S(1)} %get-tuple-element.78), channel_id=1, source_target_pairs={{1,0},{2,1},{3,2},{4,3},{5,4},{6,5},{7,6},{8,7},{9,8},{10,9},{11,1... | collective-permute-start | bytes 245768 | tf_op jit(solution)/shard_map/ppermute | solution.py:19
  39.5 5.7 %collective-permute-start.6 = (bf16[16,1,1280]{2,0,1:T(8,128)(2,1)S(1)}, bf16[16,1,1280]{2,0,1:T(8,128)(2,1)S(1)}, u32[]{:S(2)}, u32[]{:S(2)}) collective-permute-start(bf16[16,1,1280]{2,0,1:T(8,128)(2,1)S(1)} %get-tuple-element.85), channel_id=1, source_target_pairs={{0,1},{1,2},{2,3},{3,4},{4,5},{5,6},{6,7},{7,8},{8,9},{9,10},{10,1... | collective-permute-start | bytes 122888 | tf_op jit(solution)/shard_map/ppermute | solution.py:16
  43.5 5.9 %collective-permute-start.7 = (bf16[16,1,1280]{2,0,1:T(8,128)(2,1)S(1)}, bf16[16,1,1280]{2,0,1:T(8,128)(2,1)S(1)}, u32[]{:S(2)}, u32[]{:S(2)}) collective-permute-start(bf16[16,1,1280]{2,0,1:T(8,128)(2,1)S(1)} %get-tuple-element.86), channel_id=1, source_target_pairs={{1,0},{2,1},{3,2},{4,3},{5,4},{6,5},{7,6},{8,7},{9,8},{10,9},{11,1... | collective-permute-start | bytes 122888 | tf_op jit(solution)/shard_map/ppermute | solution.py:19
  54.0 1.3 copy-start
  55.4 2.8 copy-start.3
  55.4 2.9 copy-start.4
  55.4 40.3 %copy-start.8 = (f32[16,320]{1,0:T(8,128)S(1)}, f32[16,320]{1,0:T(8,128)}, u32[]{:S(2)}) copy-start(f32[16,320]{1,0:T(8,128)} %param.18) | copy-start | bytes 61444
  58.2 47.2 %copy-start.7 = (f32[1,128,8]{1,2,0:T(8,128)S(1)}, f32[1,128,8]{1,2,0:T(8,128)}, u32[]{:S(2)}) copy-start(f32[1,128,8]{1,2,0:T(8,128)} %param.24) | copy-start | bytes 12292
  58.2 48.0 %copy-start.6 = (f32[1,128,8]{1,2,0:T(8,128)S(1)}, f32[1,128,8]{1,2,0:T(8,128)}, u32[]{:S(2)}) copy-start(f32[1,128,8]{1,2,0:T(8,128)} %param.23) | copy-start | bytes 12292
  95.7 38.6 %copy-start.5 = (s32[1,128,8]{1,2,0:T(8,128)S(1)}, s32[1,128,8]{1,2,0:T(8,128)}, u32[]{:S(2)}) copy-start(s32[1,128,8]{1,2,0:T(8,128)} %param.22) | copy-start | bytes 12292
  97.9 16.9 %all-to-all-start = ((f32[128,1,8]{2,1,0:T(1,128)}), f32[128,1,8]{2,1,0:T(1,128)S(1)}, u32[]{:S(2)}, u32[]{:S(2)}) async-start(f32[128,1,8]{2,1,0:T(1,128)} %copy.126), calls=%async_computation | async-start | bytes 131072 | tf_op jit(solution)/shard_map/all_to_all | solution.py:182
  115.9 18.2 %all-to-all-start.1 = ((f32[128,8,8]{2,1,0:T(8,128)}), f32[128,8,8]{2,1,0:T(8,128)S(1)}, u32[]{:S(2)}, u32[]{:S(2)}) async-start(f32[128,8,8]{2,1,0:T(8,128)} %bitcast.22), calls=%async_computation.1 | async-start | bytes 1048576 | tf_op jit(solution)/shard_map/all_to_all | solution.py:187
  145.8 11.7 %slice-start = ((s8[6553600]{0:T(1024)(128)(4,1)}), s8[4194304]{0:T(1024)(128)(4,1)S(1)}, s32[]{:S(2)}) async-start(s8[6553600]{0:T(1024)(128)(4,1)} %bitcast.154), calls=%async_computation.7 | async-start | bytes 8388608
  147.0 10.6 %slice-start.1 = ((s8[6553600]{0:T(1024)(128)(4,1)}), s8[2359296]{0:T(1024)(128)(4,1)S(1)}, s32[]{:S(2)}) async-start(s8[6553600]{0:T(1024)(128)(4,1)} %bitcast.154), calls=%async_computation.8 | async-start | bytes 4718592
  147.0 6.2 %collective-permute-start.8 = (f32[16,1,2560]{2,0,1:T(8,128)S(1)}, f32[16,1,2560]{2,0,1:T(8,128)S(1)}, u32[]{:S(2)}, u32[]{:S(2)}) collective-permute-start(f32[16,1,2560]{2,0,1:T(8,128)S(1)} %get-tuple-element.56), channel_id=1, source_target_pairs={{0,1},{1,2},{2,3},{3,4},{4,5},{5,6},{6,7},{7,8},{8,9},{9,10},{10,1... | collective-permute-start | bytes 491528 | tf_op jit(solution)/shard_map/ppermute | solution.py:16
  149.8 7.7 %collective-permute-start.9 = (f32[16,1,2560]{2,0,1:T(8,128)S(1)}, f32[16,1,2560]{2,0,1:T(8,128)S(1)}, u32[]{:S(2)}, u32[]{:S(2)}) collective-permute-start(f32[16,1,2560]{2,0,1:T(8,128)S(1)} %get-tuple-element.55), channel_id=1, source_target_pairs={{1,0},{2,1},{3,2},{4,3},{5,4},{6,5},{7,6},{8,7},{9,8},{10,9},{11,1... | collective-permute-start | bytes 491528 | tf_op jit(solution)/shard_map/ppermute | solution.py:19
  159.7 31.1 %copy-start.1 = (f32[16,4,1280]{2,1,0:T(4,128)S(1)}, f32[16,4,1280]{2,1,0:T(4,128)}, u32[]{:S(2)}) copy-start(f32[16,4,1280]{2,1,0:T(4,128)} %param.16) | copy-start | bytes 983044
  159.7 4.5 %collective-permute-start.10 = (f32[16,1,1280]{2,0,1:T(8,128)S(1)}, f32[16,1,1280]{2,0,1:T(8,128)S(1)}, u32[]{:S(2)}, u32[]{:S(2)}) collective-permute-start(f32[16,1,1280]{2,0,1:T(8,128)S(1)} %get-tuple-element.75), channel_id=1, source_target_pairs={{0,1},{1,2},{2,3},{3,4},{4,5},{5,6},{6,7},{7,8},{8,9},{9,10},{10,1... | collective-permute-start | bytes 245768 | tf_op jit(solution)/shard_map/ppermute | solution.py:16
  162.2 6.3 %collective-permute-start.11 = (f32[16,1,1280]{2,0,1:T(8,128)S(1)}, f32[16,1,1280]{2,0,1:T(8,128)S(1)}, u32[]{:S(2)}, u32[]{:S(2)}) collective-permute-start(f32[16,1,1280]{2,0,1:T(8,128)S(1)} %get-tuple-element.76), channel_id=1, source_target_pairs={{1,0},{2,1},{3,2},{4,3},{5,4},{6,5},{7,6},{8,7},{9,8},{10,9},{11,1... | collective-permute-start | bytes 245768 | tf_op jit(solution)/shard_map/ppermute | solution.py:19
  168.6 7.4 %collective-permute-start.12 = (f32[16,1,1280]{2,0,1:T(8,128)S(1)}, f32[16,1,1280]{2,0,1:T(8,128)S(1)}, u32[]{:S(2)}, u32[]{:S(2)}) collective-permute-start(f32[16,1,1280]{2,0,1:T(8,128)S(1)} %get-tuple-element.73), channel_id=1, source_target_pairs={{0,1},{1,2},{2,3},{3,4},{4,5},{5,6},{6,7},{7,8},{8,9},{9,10},{10,1... | collective-permute-start | bytes 245768 | tf_op jit(solution)/shard_map/ppermute | solution.py:16
  174.0 6.3 %collective-permute-start.13 = (f32[16,1,1280]{2,0,1:T(8,128)S(1)}, f32[16,1,1280]{2,0,1:T(8,128)S(1)}, u32[]{:S(2)}, u32[]{:S(2)}) collective-permute-start(f32[16,1,1280]{2,0,1:T(8,128)S(1)} %get-tuple-element.74), channel_id=1, source_target_pairs={{1,0},{2,1},{3,2},{4,3},{5,4},{6,5},{7,6},{8,7},{9,8},{10,9},{11,1... | collective-permute-start | bytes 245768 | tf_op jit(solution)/shard_map/ppermute | solution.py:19
  180.4 6.1 %collective-permute-start.14 = (f32[16,1,1280]{2,0,1:T(8,128)S(1)}, f32[16,1,1280]{2,0,1:T(8,128)S(1)}, u32[]{:S(2)}, u32[]{:S(2)}) collective-permute-start(f32[16,1,1280]{2,0,1:T(8,128)S(1)} %get-tuple-element.71), channel_id=1, source_target_pairs={{0,1},{1,2},{2,3},{3,4},{4,5},{5,6},{6,7},{7,8},{8,9},{9,10},{10,1... | collective-permute-start | bytes 245768 | tf_op jit(solution)/shard_map/ppermute | solution.py:16
  184.5 6.3 %collective-permute-start.15 = (f32[16,1,1280]{2,0,1:T(8,128)S(1)}, f32[16,1,1280]{2,0,1:T(8,128)S(1)}, u32[]{:S(2)}, u32[]{:S(2)}) collective-permute-start(f32[16,1,1280]{2,0,1:T(8,128)S(1)} %get-tuple-element.72), channel_id=1, source_target_pairs={{1,0},{2,1},{3,2},{4,3},{5,4},{6,5},{7,6},{8,7},{9,8},{10,9},{11,1... | collective-permute-start | bytes 245768 | tf_op jit(solution)/shard_map/ppermute | solution.py:19
  191.5 6.1 %collective-permute-start.16 = (f32[16,1,1280]{2,0,1:T(8,128)S(1)}, f32[16,1,1280]{2,0,1:T(8,128)S(1)}, u32[]{:S(2)}, u32[]{:S(2)}) collective-permute-start(f32[16,1,1280]{2,0,1:T(8,128)S(1)} %get-tuple-element.69), channel_id=1, source_target_pairs={{0,1},{1,2},{2,3},{3,4},{4,5},{5,6},{6,7},{7,8},{8,9},{9,10},{10,1... | collective-permute-start | bytes 245768 | tf_op jit(solution)/shard_map/ppermute | solution.py:16
  195.6 6.3 %collective-permute-start.17 = (f32[16,1,1280]{2,0,1:T(8,128)S(1)}, f32[16,1,1280]{2,0,1:T(8,128)S(1)}, u32[]{:S(2)}, u32[]{:S(2)}) collective-permute-start(f32[16,1,1280]{2,0,1:T(8,128)S(1)} %get-tuple-element.70), channel_id=1, source_target_pairs={{1,0},{2,1},{3,2},{4,3},{5,4},{6,5},{7,6},{8,7},{9,8},{10,9},{11,1... | collective-permute-start | bytes 245768 | tf_op jit(solution)/shard_map/ppermute | solution.py:19
  202.0 6.1 %collective-permute-start.18 = (f32[16,1,1280]{2,0,1:T(8,128)S(1)}, f32[16,1,1280]{2,0,1:T(8,128)S(1)}, u32[]{:S(2)}, u32[]{:S(2)}) collective-permute-start(f32[16,1,1280]{2,0,1:T(8,128)S(1)} %get-tuple-element.67), channel_id=1, source_target_pairs={{0,1},{1,2},{2,3},{3,4},{4,5},{5,6},{6,7},{7,8},{8,9},{9,10},{10,1... | collective-permute-start | bytes 245768 | tf_op jit(solution)/shard_map/ppermute | solution.py:16
  206.0 6.3 %collective-permute-start.19 = (f32[16,1,1280]{2,0,1:T(8,128)S(1)}, f32[16,1,1280]{2,0,1:T(8,128)S(1)}, u32[]{:S(2)}, u32[]{:S(2)}) collective-permute-start(f32[16,1,1280]{2,0,1:T(8,128)S(1)} %get-tuple-element.68), channel_id=1, source_target_pairs={{1,0},{2,1},{3,2},{4,3},{5,4},{6,5},{7,6},{8,7},{9,8},{10,9},{11,1... | collective-permute-start | bytes 245768 | tf_op jit(solution)/shard_map/ppermute | solution.py:19
  212.4 6.4 %collective-permute-start.20 = (f32[16,1,1280]{2,0,1:T(8,128)S(1)}, f32[16,1,1280]{2,0,1:T(8,128)S(1)}, u32[]{:S(2)}, u32[]{:S(2)}) collective-permute-start(f32[16,1,1280]{2,0,1:T(8,128)S(1)} %get-tuple-element.65), channel_id=1, source_target_pairs={{0,1},{1,2},{2,3},{3,4},{4,5},{5,6},{6,7},{7,8},{8,9},{9,10},{10,1... | collective-permute-start | bytes 245768 | tf_op jit(solution)/shard_map/ppermute | solution.py:16
  216.5 6.8 %collective-permute-start.21 = (f32[16,1,1280]{2,0,1:T(8,128)S(1)}, f32[16,1,1280]{2,0,1:T(8,128)S(1)}, u32[]{:S(2)}, u32[]{:S(2)}) collective-permute-start(f32[16,1,1280]{2,0,1:T(8,128)S(1)} %get-tuple-element.66), channel_id=1, source_target_pairs={{1,0},{2,1},{3,2},{4,3},{5,4},{6,5},{7,6},{8,7},{9,8},{10,9},{11,1... | collective-permute-start | bytes 245768 | tf_op jit(solution)/shard_map/ppermute | solution.py:19
  223.3 15.3 %collective-permute-start.22 = (bf16[16,1,1280]{2,0,1:T(8,128)(2,1)S(1)}, bf16[16,1,1280]{2,0,1:T(8,128)(2,1)S(1)}, u32[]{:S(2)}, u32[]{:S(2)}) collective-permute-start(bf16[16,1,1280]{2,0,1:T(8,128)(2,1)S(1)} %get-tuple-element.83), channel_id=1, source_target_pairs={{0,1},{1,2},{2,3},{3,4},{4,5},{5,6},{6,7},{7,8},{8,9},{9,10},{10,1... | collective-permute-start | bytes 122888 | tf_op jit(solution)/shard_map/ppermute | solution.py:16
  227.4 11.2 %collective-permute-start.23 = (bf16[16,1,1280]{2,0,1:T(8,128)(2,1)S(1)}, bf16[16,1,1280]{2,0,1:T(8,128)(2,1)S(1)}, u32[]{:S(2)}, u32[]{:S(2)}) collective-permute-start(bf16[16,1,1280]{2,0,1:T(8,128)(2,1)S(1)} %get-tuple-element.84), channel_id=1, source_target_pairs={{1,0},{2,1},{3,2},{4,3},{5,4},{6,5},{7,6},{8,7},{9,8},{10,9},{11,1... | collective-permute-start | bytes 122888 | tf_op jit(solution)/shard_map/ppermute | solution.py:19
  229.6 22.5 %all-to-all-start.2 = ((f32[128,8,8]{2,1,0:T(8,128)}), f32[128,8,8]{2,1,0:T(8,128)S(1)}, u32[]{:S(2)}, u32[]{:S(2)}) async-start(f32[128,8,8]{2,1,0:T(8,128)} %bitcast.31), calls=%async_computation.2 | async-start | bytes 1048576 | tf_op jit(solution)/shard_map/all_to_all | solution.py:190
  238.5 41.7 %reduce-scatter.9.cloned.1.call-start = ((), (), s32[]{:S(2)}) async-start(), calls=%async_computation.6 | async-start | bytes 1474560
Sparse Core Ops, SparseCore 0:
  58.3 36.3 reduce-scatter.6
  246.4 33.7 reduce-scatter.8
